TPU v7x, 256 devices: a whole 4x4x8 slice. The times are simulated.
256 devices in a mesh: gx: 16 (over y_lo, z), gy: 16 (over y_hi, x, core).
Axes of the slice: x: 4, y: 4 (y_hi: 2, y_lo: 2; y = y_hi * 2 + y_lo), z: 8, core: 2. Of those that a mesh axis runs over, the one named last changes fastest.
Arguments:
- tokens: bfloat16 [8192, 2048], P('gx', 'gy'), may hold values from -40 to 40
- norm_gain: float32 [2048], replicated, may hold values from 0.25 to 1.75
- expert_ids: int32 [8192, 6], P('gx'), may hold values from 0 to 63, all different within a row; in each aligned block of 512 rows (0 to 511, 512 to 1023, ...) at most 64 rows name the same one
- gate_weights: float32 [8192, 6], P('gx'), may hold values from 0.05 to 0.35
- shared_in: bfloat16 [2, 2048, 2816], P(None, 'gx', 'gy'), may hold values from -0.125 to 0.125
- shared_out: bfloat16 [2816, 2048], P('gy', 'gx'), may hold values from -0.109375 to 0.109375
- expert_in: bfloat16 [256, 2048, 704], P(('gx', 'gy')), may hold values from -0.125 to 0.125
- expert_out: bfloat16 [256, 352, 2048], P(('gx', 'gy')), may hold values from -0.15625 to 0.15625
Outputs:
- combined: bfloat16 [8192, 2048], P('gx', 'gy')
Inputs may be any that keep to these rules, and one draw needn't show every extreme that they name: `expert_ids`: each row names 6 different experts. In each aligned block of 512 rows (the tokens of one index of gx) no expert is named by more than 64 rows, and in some block one expert is named by exactly 64.
All inputs are finite; a program needn't handle non-finite values.
Results may differ from a plain program's by a relative error of at most 0.017.
Values may be sent and summed in bfloat16 or wider, within the bound.
A program may use at most 64 MiB of HBM per device.

v0:
```python
import jax
import jax.numpy as jnp
from jax import lax
from jax.sharding import PartitionSpec as P

FF = 1408
EXPERTS = 64
CAP = 64


epsilon = 1e-06


def on_device(
    tokens, norm_gain, expert_ids, gate_weights, shared_in, shared_out, expert_in, expert_out
):
    row_count = lax.axis_size("gx")
    column_count = lax.axis_size("gy")
    column_index = lax.axis_index("gy")
    token_count = tokens.shape[0]
    top_count = expert_ids.shape[1]
    features = norm_gain.shape[0]
    held_rows = expert_in.shape[0]
    part_units = expert_out.shape[1]
    slice_count = FF // part_units
    gathered = lax.all_gather(tokens, "gy", axis=1, tiled=True)
    values = gathered.astype(jnp.float32)
    inverse_rms = lax.rsqrt(jnp.mean(values * values, axis=1, keepdims=True) + epsilon)
    normed = (values * inverse_rms * norm_gain).astype(jnp.bfloat16)
    shared_gate_up = jnp.einsum(
        "td,gdf->gtf",
        normed,
        lax.all_gather(shared_in, "gx", axis=1, tiled=True),
        preferred_element_type=jnp.float32,
    )
    shared_hidden = (jax.nn.silu(shared_gate_up[0]) * shared_gate_up[1]).astype(jnp.bfloat16)
    shared_term = jnp.dot(
        shared_hidden,
        lax.all_gather(shared_out, "gx", axis=1, tiled=True),
        preferred_element_type=jnp.float32,
    )
    flat_routes = expert_ids.reshape(-1)
    one_hot = (flat_routes[:, None] == jnp.arange(EXPERTS, dtype=jnp.int32)[None, :]).astype(
        jnp.int32
    )
    earlier_count = jnp.cumsum(one_hot, axis=0) - one_hot
    slot_index = jnp.sum(earlier_count * one_hot, axis=1)
    slice_here = column_index % slice_count
    weight_row = flat_routes * slice_count + slice_here
    owner_index = weight_row // held_rows
    on_column = owner_index % column_count == column_index
    target_row = owner_index // column_count
    member = weight_row % held_rows
    buffer_rows = row_count * held_rows * CAP
    position = (target_row * held_rows + member) * CAP + slot_index
    position = jnp.where(on_column, position, buffer_rows)
    token_number = jnp.arange(token_count * top_count, dtype=jnp.int32) // top_count
    token_slot = (
        jnp.full((buffer_rows + 1,), token_count, jnp.int32)
        .at[position]
        .set(token_number)[:buffer_rows]
    )
    padded = jnp.concatenate([normed, jnp.zeros((1, features), jnp.bfloat16)], axis=0)
    outgoing = padded[token_slot].reshape(row_count, held_rows, CAP, features)
    gate_up = jnp.einsum(
        "shcd,hdf->shcf",
        lax.all_to_all(outgoing, "gx", split_axis=0, concat_axis=0, tiled=True),
        expert_in,
        preferred_element_type=jnp.float32,
    )
    hidden = (jax.nn.silu(gate_up[..., :part_units]) * gate_up[..., part_units:]).astype(
        jnp.bfloat16
    )
    partial_value = jnp.einsum(
        "shcf,hfd->shcd", hidden, expert_out, preferred_element_type=jnp.float32
    )
    returned = lax.all_to_all(
        partial_value.astype(jnp.bfloat16), "gx", split_axis=0, concat_axis=0, tiled=True
    )
    results = returned.reshape(buffer_rows, features)
    padded_results = jnp.concatenate([results, jnp.zeros((1, features), jnp.bfloat16)], axis=0)
    place_grid = position.reshape(token_count, top_count)
    group_sum = shared_term
    for route_number in range(top_count):
        picked = padded_results[place_grid[:, route_number]].astype(jnp.float32)
        group_sum = group_sum + gate_weights[:, route_number : route_number + 1] * picked
    combined = lax.psum_scatter(
        group_sum.astype(jnp.bfloat16), "gy", scatter_dimension=1, tiled=True
    )
    return combined


def solution(mesh):
    in_specs = (
        P("gx", "gy"),
        P(),
        P("gx", None),
        P("gx", None),
        P(None, "gx", "gy"),
        P("gy", "gx"),
        P(("gx", "gy"), None, None),
        P(("gx", "gy"), None, None),
    )
    out_specs = P("gx", "gy")
    return jax.shard_map(
        on_device, mesh=mesh, in_specs=in_specs, out_specs=out_specs, check_vma=False
    )
```

profile of v0, /device:TPU:39, one launch (start us, length us, event | category | flops | bytes accessed | tf_op | source)
XLA Modules:
  0.0 489.0 jit_solution(17826437707239259932)
XLA Ops:
  8.1 1.0 copy.23
  10.3 0.9 fusion.18
  11.2 34.8 %reduce-window.6 = s32[64,24,128]{2,1,0:T(8,128)} reduce-window(s32[64,24,128]{2,1,0:T(8,128)} %fusion.18, s32[]{:T(128)} %constant.95.clone.1), window={size=1x1x128 pad=0_0x0_0x127_0}, to_apply=%region_1.2 | reduce-window | flops 24969216 | bytes 1572868 | tf_op jit(solution)/shard_map/reduce-window
  46.1 2.3 slice.92
  48.3 1.7 copy.29
  50.3 1.4 broadcast_add_fusion
  51.9 0.9 reduce_sum.25
  52.8 1.9 fusion.24
  54.7 1.1 add.164
  56.0 11.8 %scatter_custom_fusion = s32[1025]{0:T(1024)S(1)} fusion(s32[3072]{0:T(1024)S(1)} %bitcast.95, s32[3072]{0:T(1024)S(1)} %add_select_fusion.2, s32[]{:T(128)} %constant.92.clone.1), kind=kCustom, calls=%fused_computation.84 | custom fusion | bytes 4104 | tf_op jit(solution)/shard_map/scatter | solution.py:61
  68.1 2.2 fusion
  70.9 1.4 copy-done.2
  72.3 1.5 concatenate.6
  73.7 10.7 %gather_fusion = bf16[1024,2048]{1,0:T(8,128)(2,1)} fusion(bf16[513,2048]{1,0:T(8,128)(2,1)} %concatenate.6, s32[1024]{0:T(1024)S(1)} %fusion.38), kind=kCustom, calls=%fused_computation | custom fusion | bytes 8392704 | tf_op jit(solution)/shard_map/gather | solution.py:64
  84.4 101.9 %all_to_all.10 = bf16[16,1,64,2048]{3,2,1,0:T(8,128)(2,1)S(1)} all-to-all(bf16[16,1,64,2048]{3,2,1,0:T(8,128)(2,1)} %bitcast.88), channel_id=1, replica_groups=mesh['gx'=16,'gy'=16] {'gx'}, dimensions={0} | all-to-all | bytes 8388608 | tf_op jit(solution)/shard_map/all_to_all | solution.py:67
  186.3 3.4 fusion.6
  189.8 4.3 convert_bitcast_fusion
  194.1 5.3 %all-to-all-start.1 = ((bf16[16,1,64,2048]{3,2,1,0:T(8,128)(2,1)}), bf16[16,1,64,2048]{3,2,1,0:T(8,128)(2,1)}, u32[]{:S(2)}, u32[]{:S(2)}) async-start(bf16[16,1,64,2048]{3,2,1,0:T(8,128)(2,1)} %convert_bitcast_fusion), calls=%async_computation.1 | async-start | bytes 8388608 | tf_op jit(solution)/shard_map/all_to_all | solution.py:77
  200.2 0.8 fusion.25
  201.1 128.9 %all_gather.11 = bf16[176,2048]{1,0:T(8,128)(2,1)} all-gather(bf16[176,128]{1,0:T(8,128)(2,1)S(1)} %copy-done.3), channel_id=1, replica_groups=mesh['gx'=16,'gy'=16] {'gx'}, dimensions={1}, use_global_device_ids=true | all-gather | bytes 765952 | tf_op jit(solution)/shard_map/all_gather | solution.py:39
  330.0 3.8 fusion.44
  333.8 4.7 concatenate.7
  338.6 8.0 %gather_fusion.6 = bf16[512,2048]{1,0:T(8,128)(2,1)} fusion(bf16[1025,2048]{1,0:T(8,128)(2,1)} %concatenate.7, s32[1024]{0:T(1024)S(1)} %get-tuple-element.19), kind=kCustom, calls=%fused_computation.6 | custom fusion | bytes 4196352 | tf_op jit(solution)/shard_map/gather | solution.py:85
  346.5 8.0 %gather_fusion.5 = bf16[512,2048]{1,0:T(8,128)(2,1)} fusion(bf16[1025,2048]{1,0:T(8,128)(2,1)} %concatenate.7, s32[1024]{0:T(1024)S(1)} %get-tuple-element.20), kind=kCustom, calls=%fused_computation.5 | custom fusion | bytes 4196352 | tf_op jit(solution)/shard_map/gather | solution.py:85
  354.5 8.0 %gather_fusion.4 = bf16[512,2048]{1,0:T(8,128)(2,1)} fusion(bf16[1025,2048]{1,0:T(8,128)(2,1)} %concatenate.7, s32[1024]{0:T(1024)S(1)} %get-tuple-element.21), kind=kCustom, calls=%fused_computation.4 | custom fusion | bytes 4196352 | tf_op jit(solution)/shard_map/gather | solution.py:85
  362.5 8.0 %gather_fusion.3 = bf16[512,2048]{1,0:T(8,128)(2,1)} fusion(bf16[1025,2048]{1,0:T(8,128)(2,1)} %concatenate.7, s32[1024]{0:T(1024)S(1)} %get-tuple-element.22), kind=kCustom, calls=%fused_computation.3 | custom fusion | bytes 4196352 | tf_op jit(solution)/shard_map/gather | solution.py:85
  370.5 8.2 %gather_fusion.2 = bf16[512,2048]{1,0:T(8,128)(2,1)} fusion(bf16[1025,2048]{1,0:T(8,128)(2,1)} %concatenate.7, s32[1024]{0:T(1024)S(1)} %get-tuple-element.23), kind=kCustom, calls=%fused_computation.2 | custom fusion | bytes 4196352 | tf_op jit(solution)/shard_map/gather | solution.py:85
  378.7 8.0 %gather_fusion.1 = bf16[512,2048]{1,0:T(8,128)(2,1)} fusion(bf16[1025,2048]{1,0:T(8,128)(2,1)} %concatenate.7, s32[1024]{0:T(1024)S(1)} %get-tuple-element.24), kind=kCustom, calls=%fused_computation.1 | custom fusion | bytes 4196352 | tf_op jit(solution)/shard_map/gather | solution.py:85
  386.6 9.2 %add_convert_fusion = bf16[512,2048]{1,0:T(8,128)(2,1)} fusion(bf16[512,2048]{1,0:T(8,128)(2,1)} %gather_fusion.6, bf16[512,2048]{1,0:T(8,128)(2,1)} %gather_fusion.5, bf16[512,2048]{1,0:T(8,128)(2,1)} %gather_fusion.4, bf16[512,2048]{1,0:T(8,128)(2,1)} %gather_fusion.3, bf16[512,2048]{1,0:T(8,128)(2,1)} %gather_fusion.2, ...), kind=kOutput, calls=%fused_computation.15 | convolution fusion | flops 389562368 | bytes 16134144 | tf_op jit(solution)/shard_map/dot_general | solution.py:37
  395.8 3.9 copy.30
  399.8 80.1 %reduce-scatter.4.cloned.1.call-done = bf16[128,512]{1,0:T(8,128)(2,1)} async-done(((bf16[2048,512]{1,0:T(8,128)(2,1)}), bf16[128,512]{1,0:T(8,128)(2,1)}) %reduce-scatter.4.cloned.1.call-update) | async-done | bytes 131088
  479.9 1.7 copy.31
  (37 shorter events, 4.1 us)
Async XLA Ops:
  7.4 179.0 %copy-start = (bf16[1,2048,704]{1,2,0:T(8,128)(2,1)S(1)}, bf16[1,2048,704]{1,2,0:T(8,128)(2,1)}, u32[]{:S(2)}) copy-start(bf16[1,2048,704]{1,2,0:T(8,128)(2,1)} %param.14) | copy-start | bytes 8650756
  7.4 60.7 %all-gather.3.cloned.1.call-start = ((), (), s32[]{:S(2)}) async-start(), calls=%async_computation.3 | async-start | bytes 2228224 | tf_op jit(solution)/shard_map/all_gather | solution.py:26
  51.7 18.6 %copy-start.5 = (f32[2048]{0:T(1024)S(1)}, f32[2048]{0:T(1024)}, u32[]{:S(2)}) copy-start(f32[2048]{0:T(1024)} %param.9) | copy-start | bytes 24580
  68.1 2.2 copy-start.1
  70.9 1.4 copy-start.2
  186.3 3.5 copy-start.6
  194.1 7.0 %copy-start.4 = (f32[512,6]{0,1:T(8,128)S(1)}, f32[512,6]{0,1:T(8,128)}, u32[]{:S(2)}) copy-start(f32[512,6]{0,1:T(8,128)} %param.11) | copy-start | bytes 36868
  194.1 7.0 %copy-start.3 = (bf16[176,128]{1,0:T(8,128)(2,1)S(1)}, bf16[176,128]{1,0:T(8,128)(2,1)}, u32[]{:S(2)}) copy-start(bf16[176,128]{1,0:T(8,128)(2,1)} %param.13) | copy-start | bytes 135172
  194.1 139.7 %all-to-all-start.1 = ((bf16[16,1,64,2048]{3,2,1,0:T(8,128)(2,1)}), bf16[16,1,64,2048]{3,2,1,0:T(8,128)(2,1)}, u32[]{:S(2)}, u32[]{:S(2)}) async-start(bf16[16,1,64,2048]{3,2,1,0:T(8,128)(2,1)} %convert_bitcast_fusion), calls=%async_computation.1 | async-start | bytes 8388608 | tf_op jit(solution)/shard_map/all_to_all | solution.py:77
  199.4 130.6 %all-gather.5.cloned.1.call-start = ((), (), s32[]{:S(2)}) async-start(), calls=%async_computation.4 | async-start | bytes 1531904 | tf_op jit(solution)/shard_map/all_gather | solution.py:33
  200.0 279.9 %reduce-scatter.4.cloned.1.call-start = ((), (), s32[]{:S(2)}) async-start(), calls=%async_computation.5 | async-start | bytes 2228224
Sparse Core Ops, SparseCore 0:
  10.7 57.2 all-gather.2
  399.9 79.9 reduce-scatter.3
Sparse Core Ops, SparseCore 1:
  201.6 121.4 all-gather.4
where the time goes:
time: 495 us; the launch traced here: 489 us
  blocking collectives  231 us (47%)
  local copies, waits for them, and re-layouts  91.3 us (18%)
  waiting for transfers between devices  81.6 us (16%)
  other arithmetic  44 us (9%)
  matrix products  20.8 us (4%)
  between operations  15 us (3%)
  starting transfers between devices  5.55 us (1%)
    all_gather x1, blocking collectives, on_device(): lax.all_gather(shared_out, 'gx', axis=1, tiled=True)  129 us
    all_to_all x1, blocking collectives, on_device(): lax.all_to_all(outgoing, 'gx', split_axis=0, concat_axis=0, tiled=True)  102 us
    unnamed x4, waiting for transfers between devices  81.4 us
    gather x6, local copies, waits for them, and re-layouts, on_device(): picked = padded_results[place_grid[:, route_number]].astype(jnp.float32)  48.1 us
    another operation x3, other arithmetic  36.4 us
    scatter x1, local copies, waits for them, and re-layouts, on_device(): token_slot = jnp.full((buffer_rows + 1,), token_count, jnp.int32).at[posi...  11.8 us
    gather x1, local copies, waits for them, and re-layouts, on_device(): outgoing = padded[token_slot].reshape(row_count, held_rows, CAP, features)  10.7 us
  transfers between devices with their start and end apart: 4, of which 2 were waited for; matrix products, arithmetic and copies ran while one was open for 13% of the time, Pallas kernels for 0%

commit v1 on v0

v1 whole, which is shorter than its diff:
```python
import jax
import jax.numpy as jnp
from jax import lax
from jax.experimental import pallas as pl
from jax.experimental.pallas import tpu as pltpu
from jax.sharding import PartitionSpec as P

MESH = pl.DeviceIdType.MESH
F32 = jnp.float32
BF16 = jnp.bfloat16
EPSILON = 1e-06

NX = 16
NY = 16
CAP = 64
TOK = 512
D = 2048
B = 128
Q = 512
TOPK = 6
PART = 352
SPART = 176
CH = 256
VMEM_LIMIT = 60 * 1024 * 1024


def kernel(
    tok, gain, idst, gatet, shin, shout, win_hbm, wout_hbm, out,
    xall, win, wout, wsin, wsout, code, gm, oh, og, snd, rx, xn, sa, sibin, po, pn, sn, nbrin, ret, back,
    acc, fs, fin, ssa, ssin, spo, spn, sb, shr,
    ld_sem, tok_s, tok_r, tf_s, tf_r, wz_s, wz_r, wy_s, wy_r, dp_s, dp_r, nb_s, nb_r, sq_s, sq_r,
    ra_s, ra_r, rb_s, rb_r, bk_s, bk_r, xs_s, xs_r, sr_s, sr_r, fn_s, fn_r,
):
    gx = lax.axis_index("gx")
    gy = lax.axis_index("gy")
    j, q = gy // 4, gy % 4
    ylo, z = gx // 8, gx % 8
    sib = gy + 1 - 2 * (gy % 2)
    nbr = gy + 2 - 4 * ((gy // 2) % 2)
    qs, qn = sib % 4, nbr % 4
    qsn = (qs + 2) % 4
    ypart = (gx + 8) % NX

    def peer(r):
        return (gy + r) % NY

    def remote(src, dst, send, recv, tx, ty):
        return pltpu.make_async_remote_copy(
            src_ref=src, dst_ref=dst, send_sem=send, recv_sem=recv,
            device_id=(tx, ty), device_id_type=MESH,
        )

    def shift(k, u):
        return 4 * u + (k + 3) % 4

    def loads():
        for i in range(16):
            p = (i % 4) * 4 + i // 4
            yield pltpu.make_async_copy(
                win_hbm.at[pl.ds(i * B, B), :], win.at[pl.ds(p * B, B), :], ld_sem.at[0, i]
            )
            yield pltpu.make_async_copy(
                wout_hbm.at[:, pl.ds(i * B, B)], wout.at[i % 4, :, pl.ds((i // 4) * B, B)], ld_sem.at[1, i]
            )

    for copy in loads():
        copy.start()

    barrier = pltpu.get_barrier_semaphore()
    for r in range(1, NX):
        pl.semaphore_signal(barrier, inc=1, device_id=((gx + r) % NX, gy), device_id_type=MESH)
    for r in range(1, 8):
        pl.semaphore_signal(barrier, inc=1, device_id=(gx, peer(2 * r)), device_id_type=MESH)
    pl.semaphore_signal(barrier, inc=1, device_id=(gx, sib), device_id_type=MESH)
    pl.semaphore_wait(barrier, NX - 1 + 8)

    def tok_at(owner):
        return xall.at[owner % 4, :, pl.ds(pl.multiple_of((owner // 4) * B, B), B)]

    def tok_send(r):
        return remote(tok, tok_at(gy), tok_s.at[r], tok_r.at[r], gx, peer(2 * r))

    def tok_recv(r):
        place = tok_at(peer(16 - 2 * r))
        return remote(place, place, tok_s.at[r], tok_r.at[r], gx, sib)

    def tok_forward(r):
        place = tok_at(peer(16 - 2 * r))
        return remote(place, place, tf_s.at[r], tf_r.at[r], gx, sib)

    def tok_forwarded(r):
        place = tok_at((sib + 16 - 2 * r) % NY)
        return remote(place, place, tf_s.at[r], tf_r.at[r], gx, sib)

    tok_own = remote(tok, tok_at(gy), tf_s.at[0], tf_r.at[0], gx, sib)
    for r in (2, 4, 6):
        tok_send(r).start()

    def block_z(e):
        if e == 0:
            return z
        step = (e + 1) // 2
        return (z + 8 - step) % 8 if e % 2 else (z + step) % 8

    def w_at(owner):
        place = (owner % 4) * 4 + owner // 4
        return (
            wsin.at[:, pl.ds(pl.multiple_of(place * B, B), B), :],
            wsout.at[owner % 4, :, pl.ds(pl.multiple_of((owner // 4) * B, B), B)],
        )

    def w_source(e):
        return (shin, shout) if e == 0 else w_at(ylo * 8 + block_z(e))

    def w_ring(e):
        origin = 0 if e <= 2 else e - 2
        target = ylo * 8 + ((z + 1) % 8 if e % 2 else (z + 7) % 8)
        to = w_at(ylo * 8 + block_z(origin))
        return [
            remote(w_source(origin)[t], to[t], wz_s.at[t, e], wz_r.at[t, e], target, gy) for t in range(2)
        ]

    def w_ring_recv(e):
        place = w_at(ylo * 8 + block_z(e))
        return [remote(place[t], place[t], wz_s.at[t, e], wz_r.at[t, e], ypart, gy) for t in range(2)]

    def w_cross(e):
        to = w_at(ylo * 8 + block_z(e))
        return [remote(w_source(e)[t], to[t], wy_s.at[t, e], wy_r.at[t, e], ypart, gy) for t in range(2)]

    def w_cross_recv(e):
        place = w_at((1 - ylo) * 8 + block_z(e))
        return [remote(place[t], place[t], wy_s.at[t, e], wy_r.at[t, e], ypart, gy) for t in range(2)]

    def start(copies):
        for copy in copies:
            copy.start()

    def arrived(copies):
        for copy in copies:
            copy.wait_recv()

    start(w_ring(1))
    start(w_ring(2))
    tok_own.start()
    for r in (1, 3, 5, 7):
        tok_send(r).start()
    start(w_cross(0))

    xall[q, :, pl.ds(pl.multiple_of(j * B, B), B)] = tok[...]
    wsin[:, pl.ds(pl.multiple_of(((gx % 4) * 4 + gx // 4) * B, B), B), :] = shin[...]
    wsout[gx % 4, :, pl.ds(pl.multiple_of((gx // 4) * B, B), B)] = shout[...]

    expert = 4 * lax.broadcasted_iota(jnp.int32, (NX, TOK), 0) + j
    named = jnp.zeros((NX, TOK), F32)
    weight = jnp.zeros((NX, TOK), F32)
    for k in range(TOPK):
        hit = idst[k : k + 1, :] == expert
        named = jnp.where(hit, 1.0, named)
        weight = jnp.where(hit, gatet[k : k + 1, :], weight)
    before = (
        lax.broadcasted_iota(jnp.int32, (TOK, TOK), 0) < lax.broadcasted_iota(jnp.int32, (TOK, TOK), 1)
    )
    count = jnp.dot(
        named.astype(BF16), jnp.where(before, 1.0, 0.0).astype(BF16), preferred_element_type=F32
    )
    code[...] = jnp.where(named > 0.0, count, -1.0)
    gm[...] = weight
    slot = lax.broadcasted_iota(jnp.int32, (CAP, TOK), 0).astype(F32)

    def build(k, carry):
        for u in range(4):
            m = (gx + shift(k, u)) % NX
            hit = slot == code[pl.ds(m, 1), :]
            at = pl.multiple_of((4 * k + u) * CAP, CAP)
            oh[pl.ds(at, CAP), :] = jnp.where(hit, 1.0, 0.0).astype(BF16)
            og[pl.ds(at, CAP), :] = jnp.where(hit, gm[pl.ds(m, 1), :], 0.0).astype(BF16)
        return carry

    lax.fori_loop(0, 4, build, 0)

    def slots_of(k, u):
        return pl.ds(pl.multiple_of((4 * k + u) * CAP, CAP), CAP)

    def chunk_of(k):
        return pl.ds(pl.multiple_of(k * CH, CH), CH)

    def dp(k, u):
        return remote(
            snd.at[slots_of(k, u), :], rx.at[q, slots_of(k, u), :],
            dp_s.at[4 * k + u], dp_r.at[4 * k + u], (gx + shift(k, u)) % NX, gy,
        )

    def when_self(k, u, own, other):
        if u == 0:
            pl.when(k == 1)(own)
            pl.when(k != 1)(other)
        else:
            other()

    for r in (2, 4, 6):
        tok_recv(r).wait_recv()

    def dispatch(k, carry):
        picked = jnp.dot(oh[chunk_of(k), :], xall[q], preferred_element_type=F32)
        snd[chunk_of(k), :] = picked.astype(BF16)
        for u in range(4):
            def own(u=u):
                pltpu.make_async_copy(
                    snd.at[slots_of(k, u), :], rx.at[q, slots_of(k, u), :], dp_r.at[4 * k + u]
                ).start()

            when_self(k, u, own, lambda u=u: dp(k, u).start())
        return carry

    lax.fori_loop(0, 4, dispatch, 0)

    for e in (1, 2):
        arrived(w_ring_recv(e))
        start(w_ring(e + 2))
        start(w_cross(e))
    for r in (2, 4, 6):
        tok_forward(r).start()
    for r in (1, 3, 5, 7):
        tok_recv(r).wait_recv()
        tok_forward(r).start()
    for e in (3, 4):
        arrived(w_ring_recv(e))
        start(w_ring(e + 2))
        start(w_cross(e))

    def to_nbr(k):
        place = rx.at[q, chunk_of(k), :]
        return remote(place, place, nb_s.at[k], nb_r.at[k], gx, nbr)

    def from_nbr(k):
        place = rx.at[qn, chunk_of(k), :]
        return remote(place, place, nb_s.at[k], nb_r.at[k], gx, nbr)

    def to_sib(t, k):
        place = rx.at[q if t == 0 else qn, chunk_of(k), :]
        return remote(place, place, sq_s.at[t, k], sq_r.at[t, k], gx, sib)

    def from_sib(t, k):
        place = rx.at[qs if t == 0 else qsn, chunk_of(k), :]
        return remote(place, place, sq_s.at[t, k], sq_r.at[t, k], gx, sib)

    def stage_a(k):
        for u in range(4):
            place = rx.at[q, slots_of(k, u), :]
            remote(place, place, dp_s.at[4 * k + u], dp_r.at[4 * k + u], gx, sib).wait_recv()
        to_nbr(k).start()
        to_sib(0, k).start()

    def stage_a2(k):
        from_nbr(k).wait_recv()
        to_sib(1, k).start()

    def ra(k):
        return remote(sa.at[k], sibin.at[k], ra_s.at[k], ra_r.at[k], gx, sib)

    def rb(k):
        return remote(sn.at[k], nbrin.at[k], rb_s.at[k], rb_r.at[k], gx, nbr)

    def bk(k, u):
        return remote(
            ret.at[slots_of(k, u), :], back.at[slots_of(k, u), :],
            bk_s.at[4 * k + u], bk_r.at[4 * k + u], (gx + NX - shift(k, u)) % NX, gy,
        )

    def normalise(source, rows):
        total = jnp.zeros((CH, B), F32)
        for c in range(4):
            for b in range(4):
                value = source[c, rows, b * B : (b + 1) * B].astype(F32)
                total = total + value * value
        inverse = lax.rsqrt(jnp.sum(total, axis=1, keepdims=True) * (1.0 / D) + EPSILON)
        for c in range(4):
            value = source[c, rows, :].astype(F32)
            xn[:, c * Q : (c + 1) * Q] = (value * inverse * gain[c]).astype(BF16)

    def stage_b(k):
        from_sib(0, k).wait_recv()
        from_sib(1, k).wait_recv()
        normalise(rx, chunk_of(k))
        gate_up = jnp.dot(xn[...], win[...], preferred_element_type=F32)
        hidden = (jax.nn.silu(gate_up[:, :PART]) * gate_up[:, PART:]).astype(BF16)
        sa[k, 0] = jnp.dot(hidden, wout[qs], preferred_element_type=F32).astype(BF16)
        sa[k, 1] = jnp.dot(hidden, wout[qsn], preferred_element_type=F32).astype(BF16)
        ra(k).start()
        pn[k % 2] = jnp.dot(hidden, wout[qn], preferred_element_type=F32)
        po[k % 2] = jnp.dot(hidden, wout[q], preferred_element_type=F32)

    def stage_rb(k):
        remote(sa.at[k], sibin.at[k], ra_s.at[k], ra_r.at[k], gx, sib).wait_recv()
        sn[k] = (pn[k % 2] + sibin[k, 1].astype(F32)).astype(BF16)
        rb(k).start()
        po[k % 2] = po[k % 2] + sibin[k, 0].astype(F32)

    def stage_c(k):
        remote(sn.at[k], nbrin.at[k], rb_s.at[k], rb_r.at[k], gx, nbr).wait_recv()
        ret[chunk_of(k), :] = (po[k % 2] + nbrin[k].astype(F32)).astype(BF16)
        for u in range(4):
            def own(u=u):
                pltpu.make_async_copy(
                    ret.at[slots_of(k, u), :], back.at[slots_of(k, u), :], bk_r.at[4 * k + u]
                ).start()

            when_self(k, u, own, lambda u=u: bk(k, u).start())

    stage_a(0)
    for e in (5, 6):
        arrived(w_ring_recv(e))
        if e == 5:
            start(w_ring(7))
        start(w_cross(e))
    for copy in loads():
        copy.wait()

    def routed(it, carry):
        @pl.when(it < 3)
        def _():
            stage_a(it + 1)

        @pl.when(it < 4)
        def _():
            stage_a2(it)

        @pl.when(it > 0)
        def _():
            stage_rb(it - 1)

        @pl.when(it < 4)
        def _():
            stage_b(it)

        @pl.when(it > 0)
        def _():
            stage_c(it - 1)

        return carry

    lax.fori_loop(0, 5, routed, 0)

    arrived(w_ring_recv(7))
    start(w_cross(7))
    tok_forwarded(0).wait_recv()
    for r in range(1, 8):
        tok_forwarded(r).wait_recv()
    for e in range(8):
        arrived(w_cross_recv(e))

    def shared(c, carry):
        rows = chunk_of(c)
        normalise(xall, rows)
        gate = jnp.dot(xn[...], wsin[0], preferred_element_type=F32)
        up = jnp.dot(xn[...], wsin[1], preferred_element_type=F32)
        hidden = (jax.nn.silu(gate) * up).astype(BF16)
        ssa[0, rows, :] = jnp.dot(hidden, wsout[qs], preferred_element_type=F32).astype(BF16)
        ssa[1, rows, :] = jnp.dot(hidden, wsout[qsn], preferred_element_type=F32).astype(BF16)
        spo[rows, :] = jnp.dot(hidden, wsout[q], preferred_element_type=F32)
        spn[rows, :] = jnp.dot(hidden, wsout[qn], preferred_element_type=F32)
        return carry

    lax.fori_loop(0, 2, shared, 0)
    xs = remote(ssa, ssin, xs_s.at[0], xs_r.at[0], gx, sib)
    xs.start()
    xs.wait_recv()

    def fold(c, carry):
        rows = chunk_of(c)
        own = spo[rows, :] + ssin[0, rows, :].astype(F32)
        spo[rows, :] = own
        sb[0, rows, :] = own.astype(BF16)
        sb[1, rows, :] = (spn[rows, :] + ssin[1, rows, :].astype(F32)).astype(BF16)
        return carry

    lax.fori_loop(0, 2, fold, 0)

    def sr(r):
        target = peer(2 * r)
        return remote(
            sb.at[r % 2, :, pl.ds(pl.multiple_of((target // 4) * B, B), B)], shr.at[r],
            sr_s.at[r], sr_r.at[r], gx, target,
        )

    for r in range(1, 8):
        sr(r).start()

    acc[...] = jnp.zeros((TOK, Q), F32)

    def combine(k, carry):
        for u in range(4):
            bk(k, u).wait_recv()
        acc[...] += lax.dot_general(
            og[chunk_of(k), :], back[chunk_of(k), :], (((0,), (0,)), ((), ())), preferred_element_type=F32
        )
        return carry

    lax.fori_loop(0, 4, combine, 0)

    def fn(t):
        return remote(fs.at[t], fin.at[t], fn_s.at[t], fn_r.at[t], gx, peer(4 * t))

    for t in range(1, 4):
        at = pl.multiple_of(((j + t) % 4) * B, B)
        fs[t] = acc[:, pl.ds(at, B)].astype(BF16)
        fn(t).start()
    mine = pl.ds(pl.multiple_of(j * B, B), B)
    total = acc[:, mine] + spo[:, mine]
    for r in range(1, 8):
        sr(r).wait_recv()
        total = total + shr[r].astype(F32)
    for t in range(1, 4):
        fn(t).wait_recv()
        total = total + fin[t].astype(F32)
    out[...] = total.astype(BF16)

    tok_own.wait_send()
    for r in range(1, 8):
        tok_send(r).wait_send()
        tok_forward(r).wait_send()
        sr(r).wait_send()
        for copy in w_ring(r):
            copy.wait_send()
    for e in range(8):
        for copy in w_cross(e):
            copy.wait_send()
    xs.wait_send()
    for t in range(1, 4):
        fn(t).wait_send()

    def drain(k, carry):
        to_nbr(k).wait_send()
        to_sib(0, k).wait_send()
        to_sib(1, k).wait_send()
        ra(k).wait_send()
        rb(k).wait_send()
        for u in range(4):
            def both(u=u):
                dp(k, u).wait_send()
                bk(k, u).wait_send()

            when_self(k, u, lambda: None, both)
        return carry

    lax.fori_loop(0, 4, drain, 0)


def on_device(tokens, norm_gain, expert_ids, gate_weights, shared_in, shared_out, expert_in, expert_out):
    gain = norm_gain.reshape(4, 4, B).transpose(1, 0, 2).reshape(4, 1, Q)
    dma = pltpu.SemaphoreType.DMA
    vmem = pl.BlockSpec(memory_space=pltpu.VMEM)
    anywhere = pl.BlockSpec(memory_space=pl.ANY)
    return pl.pallas_call(
        kernel,
        out_shape=jax.ShapeDtypeStruct((TOK, B), BF16),
        in_specs=[vmem] * 6 + [anywhere] * 2,
        out_specs=vmem,
        scratch_shapes=[
            pltpu.VMEM((4, TOK, Q), BF16),
            pltpu.VMEM((D, 2 * PART), BF16),
            pltpu.VMEM((4, PART, Q), BF16),
            pltpu.VMEM((2, D, SPART), BF16),
            pltpu.VMEM((4, SPART, Q), BF16),
            pltpu.VMEM((NX, TOK), F32),
            pltpu.VMEM((NX, TOK), F32),
            pltpu.VMEM((NX * CAP, TOK), BF16),
            pltpu.VMEM((NX * CAP, TOK), BF16),
            pltpu.VMEM((NX * CAP, Q), BF16),
            pltpu.VMEM((4, NX * CAP, Q), BF16),
            pltpu.VMEM((CH, D), BF16),
            pltpu.VMEM((4, 2, CH, Q), BF16),
            pltpu.VMEM((4, 2, CH, Q), BF16),
            pltpu.VMEM((2, CH, Q), F32),
            pltpu.VMEM((2, CH, Q), F32),
            pltpu.VMEM((4, CH, Q), BF16),
            pltpu.VMEM((4, CH, Q), BF16),
            pltpu.VMEM((NX * CAP, Q), BF16),
            pltpu.VMEM((NX * CAP, Q), BF16),
            pltpu.VMEM((TOK, Q), F32),
            pltpu.VMEM((4, TOK, B), BF16),
            pltpu.VMEM((4, TOK, B), BF16),
            pltpu.VMEM((2, TOK, Q), BF16),
            pltpu.VMEM((2, TOK, Q), BF16),
            pltpu.VMEM((TOK, Q), F32),
            pltpu.VMEM((TOK, Q), F32),
            pltpu.VMEM((2, TOK, Q), BF16),
            pltpu.VMEM((8, TOK, B), BF16),
            dma((2, 16)),
            dma((8,)), dma((8,)),
            dma((8,)), dma((8,)),
            dma((2, 8)), dma((2, 8)),
            dma((2, 8)), dma((2, 8)),
            dma((16,)), dma((16,)),
            dma((4,)), dma((4,)),
            dma((2, 4)), dma((2, 4)),
            dma((4,)), dma((4,)),
            dma((4,)), dma((4,)),
            dma((16,)), dma((16,)),
            dma((1,)), dma((1,)),
            dma((8,)), dma((8,)),
            dma((4,)), dma((4,)),
        ],
        compiler_params=pltpu.CompilerParams(
            collective_id=0, has_side_effects=True, vmem_limit_bytes=VMEM_LIMIT
        ),
    )(
        tokens, gain, expert_ids.T, gate_weights.T, shared_in, shared_out,
        expert_in.reshape(D, 2 * PART), expert_out.reshape(PART, D),
    )


def solution(mesh):
    in_specs = (
        P("gx", "gy"),
        P(),
        P("gx", None),
        P("gx", None),
        P(None, "gx", "gy"),
        P("gy", "gx"),
        P(("gx", "gy"), None, None),
        P(("gx", "gy"), None, None),
    )
    return jax.shard_map(
        on_device, mesh=mesh, in_specs=in_specs, out_specs=P("gx", "gy"), check_vma=False
    )
```

time: 495 us -> 154 us (0.31); the launches traced: 489 us -> 154 us
  blocking collectives: 231 us -> 0 us
  Pallas kernels: 0 us -> 145 us
  local copies, waits for them, and re-layouts: 91.3 us -> 9.11 us
  waiting for transfers between devices: 81.6 us -> 0 us
  other arithmetic: 44 us -> 0 us
  matrix products: 20.8 us -> 0 us
  between operations: 15 us -> 0.01 us
  starting transfers between devices: 5.55 us -> 0 us
    pallas_call x0 -> x1, Pallas kernels: none -> 145 us  [on_device(): pl.pallas_call(kernel, out_shape=jax.ShapeDtypeStruct((TOK, B), BF16), in...]
    all_gather x1 -> x0, blocking collectives: 129 us -> none  [on_device(): lax.all_gather(shared_out, 'gx', axis=1, tiled=True)]
    all_to_all x1 -> x0, blocking collectives: 102 us -> none  [on_device(): lax.all_to_all(outgoing, 'gx', split_axis=0, concat_axis=0, tiled=True)]
    unnamed x4 -> x0, waiting for transfers between devices: 81.4 us -> none
    gather x7 -> x0, local copies, waits for them, and re-layouts: 58.8 us -> none  [the longest x6 48.1 us: on_device(): picked = padded_results[place_grid[:, route_number]].astype(jnp.float32)]
    another operation x3 -> x0, other arithmetic: 36.4 us -> none
    dot_general x3 -> x0, matrix products: 17 us -> none  [the longest x1 9.2 us: on_device(): jnp.dot(shared_hidden, lax.all_gather(shared_out, 'gx', axis=1, tiled=Tru...]
    scatter x1 -> x0, local copies, waits for them, and re-layouts: 11.8 us -> none  [on_device(): token_slot = jnp.full((buffer_rows + 1,), token_count, jnp.int32).at[posi...]
  transfers between devices with their start and end apart: 4 -> 0, of which waited for: 2 -> 0; matrix products, arithmetic and copies ran while one was open for 13% -> 0% of each run, Pallas kernels for 0% -> 0%
where the time goes in v1:
time: 154 us
  Pallas kernels  145 us (94%)
  local copies, waits for them, and re-layouts  9.11 us (6%)
    pallas_call x1, Pallas kernels, on_device(): pl.pallas_call(kernel, out_shape=jax.ShapeDtypeStruct((TOK, B), BF16), in...  145 us
    unnamed x3, local copies, waits for them, and re-layouts  7.81 us

profile of v1, /device:TPU:39, one launch (start us, length us, event | category | flops | bytes accessed | tf_op | source)
XLA Modules:
  0.0 153.7 jit_solution(12511649460695609608)
XLA Ops:
  0.0 1.3 copy.11
  1.3 1.6 %copy.13.shin = bf16[2,128,176]{2,1,0:T(8,128)(2,1)} copy(bf16[2,128,176]{1,2,0:T(8,128)(2,1)} %param.12) | data formatting | bytes 180224 | tf_op args[4]
  2.9 4.6 %copy.12 = bf16[1,2048,704]{2,1,0:T(8,128)(2,1)} copy(bf16[1,2048,704]{1,2,0:T(8,128)(2,1)} %param.14) | data formatting | bytes 5767168 | tf_op args[6]
  7.5 144.6 %shard_map.82 = bf16[512,128]{1,0:T(8,128)(2,1)} custom-call(bf16[512,128]{1,0:T(8,128)(2,1)} %tok.1, f32[4,1,512]{2,1,0:T(1,128)} %bitcast.10, s32[6,512]{1,0:T(8,128)} %bitcast.11, f32[6,512]{1,0:T(8,128)} %bitcast.12, bf16[2,128,176]{2,1,0:T(8,128)(2,1)} %copy.13.shin, bf16[176,128]{1,0:T(8,128)(2,1)} %shout.1, bf16[2048,704]{1,0:T(8,128)(2,1)} %bitcast.8, ...), custom_call_target="tpu_custom_call" | custom-call | tf_op jit(solution)/shard_map/pallas_call | solution.py:455
  152.2 1.6 %copy.15 = bf16[512,128]{1,0:T(8,128)(2,1)} copy(bf16[512,128]{1,0:T(8,128)(2,1)} %shard_map.82) | data formatting | bytes 262144

commit v2 on v1

--- a/solution.py
+++ b/solution.py
@@ -57,7 +57,7 @@
         for i in range(16):
             p = (i % 4) * 4 + i // 4
             yield pltpu.make_async_copy(
-                win_hbm.at[pl.ds(i * B, B), :], win.at[pl.ds(p * B, B), :], ld_sem.at[0, i]
+                win_hbm.at[:, pl.ds(i * B, B)], win.at[:, pl.ds(p * B, B)], ld_sem.at[0, i]
             )
             yield pltpu.make_async_copy(
                 wout_hbm.at[:, pl.ds(i * B, B)], wout.at[i % 4, :, pl.ds((i // 4) * B, B)], ld_sem.at[1, i]
@@ -105,7 +105,7 @@
     def w_at(owner):
         place = (owner % 4) * 4 + owner // 4
         return (
-            wsin.at[:, pl.ds(pl.multiple_of(place * B, B), B), :],
+            wsin.at[:, :, pl.ds(pl.multiple_of(place * B, B), B)],
             wsout.at[owner % 4, :, pl.ds(pl.multiple_of((owner // 4) * B, B), B)],
         )
 
@@ -148,7 +148,7 @@
     start(w_cross(0))
 
     xall[q, :, pl.ds(pl.multiple_of(j * B, B), B)] = tok[...]
-    wsin[:, pl.ds(pl.multiple_of(((gx % 4) * 4 + gx // 4) * B, B), B), :] = shin[...]
+    wsin[:, :, pl.ds(pl.multiple_of(((gx % 4) * 4 + gx // 4) * B, B), B)] = shin[...]
     wsout[gx % 4, :, pl.ds(pl.multiple_of((gx // 4) * B, B), B)] = shout[...]
 
     expert = 4 * lax.broadcasted_iota(jnp.int32, (NX, TOK), 0) + j
@@ -268,6 +268,9 @@
             bk_s.at[4 * k + u], bk_r.at[4 * k + u], (gx + NX - shift(k, u)) % NX, gy,
         )
 
+    def dot_nt(a, b):
+        return lax.dot_general(a, b, (((1,), (1,)), ((), ())), preferred_element_type=F32)
+
     def normalise(source, rows):
         total = jnp.zeros((CH, B), F32)
         for c in range(4):
@@ -276,15 +279,17 @@
                 total = total + value * value
         inverse = lax.rsqrt(jnp.sum(total, axis=1, keepdims=True) * (1.0 / D) + EPSILON)
         for c in range(4):
-            value = source[c, rows, :].astype(F32)
-            xn[:, c * Q : (c + 1) * Q] = (value * inverse * gain[c]).astype(BF16)
+            for b in range(4):
+                value = source[c, rows, b * B : (b + 1) * B].astype(F32)
+                scaled = value * inverse * gain[4 * b + c : 4 * b + c + 1, :]
+                xn[:, c * Q + b * B : c * Q + (b + 1) * B] = scaled.astype(BF16)
 
     def stage_b(k):
         from_sib(0, k).wait_recv()
         from_sib(1, k).wait_recv()
         normalise(rx, chunk_of(k))
-        gate_up = jnp.dot(xn[...], win[...], preferred_element_type=F32)
-        hidden = (jax.nn.silu(gate_up[:, :PART]) * gate_up[:, PART:]).astype(BF16)
+        gate, up = dot_nt(xn[...], win[:PART, :]), dot_nt(xn[...], win[PART:, :])
+        hidden = (jax.nn.silu(gate) * up).astype(BF16)
         sa[k, 0] = jnp.dot(hidden, wout[qs], preferred_element_type=F32).astype(BF16)
         sa[k, 1] = jnp.dot(hidden, wout[qsn], preferred_element_type=F32).astype(BF16)
         ra(k).start()
@@ -353,8 +358,7 @@
     def shared(c, carry):
         rows = chunk_of(c)
         normalise(xall, rows)
-        gate = jnp.dot(xn[...], wsin[0], preferred_element_type=F32)
-        up = jnp.dot(xn[...], wsin[1], preferred_element_type=F32)
+        gate, up = dot_nt(xn[...], wsin[0]), dot_nt(xn[...], wsin[1])
         hidden = (jax.nn.silu(gate) * up).astype(BF16)
         ssa[0, rows, :] = jnp.dot(hidden, wsout[qs], preferred_element_type=F32).astype(BF16)
         ssa[1, rows, :] = jnp.dot(hidden, wsout[qsn], preferred_element_type=F32).astype(BF16)
@@ -448,7 +452,6 @@
 
 
 def on_device(tokens, norm_gain, expert_ids, gate_weights, shared_in, shared_out, expert_in, expert_out):
-    gain = norm_gain.reshape(4, 4, B).transpose(1, 0, 2).reshape(4, 1, Q)
     dma = pltpu.SemaphoreType.DMA
     vmem = pl.BlockSpec(memory_space=pltpu.VMEM)
     anywhere = pl.BlockSpec(memory_space=pl.ANY)
@@ -459,9 +462,9 @@
         out_specs=vmem,
         scratch_shapes=[
             pltpu.VMEM((4, TOK, Q), BF16),
-            pltpu.VMEM((D, 2 * PART), BF16),
+            pltpu.VMEM((2 * PART, D), BF16),
             pltpu.VMEM((4, PART, Q), BF16),
-            pltpu.VMEM((2, D, SPART), BF16),
+            pltpu.VMEM((2, SPART, D), BF16),
             pltpu.VMEM((4, SPART, Q), BF16),
             pltpu.VMEM((NX, TOK), F32),
             pltpu.VMEM((NX, TOK), F32),
@@ -506,8 +509,9 @@
             collective_id=0, has_side_effects=True, vmem_limit_bytes=VMEM_LIMIT
         ),
     )(
-        tokens, gain, expert_ids.T, gate_weights.T, shared_in, shared_out,
-        expert_in.reshape(D, 2 * PART), expert_out.reshape(PART, D),
+        tokens, norm_gain.reshape(D // B, B), expert_ids.T, gate_weights.T,
+        jnp.swapaxes(shared_in, 1, 2), shared_out,
+        expert_in.reshape(D, 2 * PART).T, expert_out.reshape(PART, D),
     )
 
 

time: 154 us -> 148 us (0.961)
  the two profiles are of different devices: /device:TPU:39 before, /device:TPU:37 now
where the time goes in v2:
time: 148 us
  Pallas kernels  146 us (99%)
  local copies, waits for them, and re-layouts  1.57 us (1%)
    pallas_call x1, Pallas kernels, on_device(): pl.pallas_call(kernel, out_shape=jax.ShapeDtypeStruct((TOK, B), BF16), in...  146 us

profile of v2, /device:TPU:37, one launch (start us, length us, event | category | flops | bytes accessed | tf_op | source)
XLA Modules:
  0.0 147.5 jit_solution(16227600402513966450)
XLA Ops:
  0.0 145.9 %shard_map.82 = bf16[512,128]{1,0:T(8,128)(2,1)} custom-call(bf16[512,128]{1,0:T(8,128)(2,1)} %tok.1, f32[16,128]{1,0:T(8,128)} %bitcast.13, s32[6,512]{1,0:T(8,128)} %bitcast.11, f32[6,512]{1,0:T(8,128)} %bitcast.12, bf16[2,176,128]{2,1,0:T(8,128)(2,1)} %bitcast.10, bf16[176,128]{1,0:T(8,128)(2,1)} %shout.1, bf16[704,2048]{1,0:T(8,128)(2,1)} %bitcast.8, ...), custom_call_target="tpu_custom_call" | custom-call | tf_op jit(solution)/shard_map/pallas_call | solution.py:458
  145.9 1.6 %copy.10 = bf16[512,128]{1,0:T(8,128)(2,1)} copy(bf16[512,128]{1,0:T(8,128)(2,1)} %shard_map.82) | data formatting | bytes 262144

commit v3 on v2

v3 whole, which is shorter than its diff:
```python
import jax
import jax.numpy as jnp
from jax import lax
from jax.experimental import pallas as pl
from jax.experimental.pallas import tpu as pltpu
from jax.sharding import PartitionSpec as P

MESH = pl.DeviceIdType.MESH
F32 = jnp.float32
BF16 = jnp.bfloat16
EPSILON = 1e-06

NX = 16
NY = 16
CAP = 64
TOK = 512
D = 2048
B = 128
Q = 512
TOPK = 6
PART = 352
SPART = 176
NS = 2
NC = NX // NS
CH = NS * CAP
SELF = 4 if NS == 2 else 1
SH = 256
VMEM_LIMIT = 60 * 1024 * 1024


def kernel(
    tok, gain, idst, gatet, shin, shout, win_hbm, wout_hbm, out,
    xall, win, wout, wsin, wsout, code, gm, oh, og, snd, rx, xn, sa, sibin, po, pn, sn, nbrin, ret, back,
    acc, fs, fin, ssa, ssin, spo, spn, sb, shr,
    ld_sem, tok_s, tok_r, tf_s, tf_r, wz_s, wz_r, wy_s, wy_r, dp_s, dp_r, nb_s, nb_r, sq_s, sq_r,
    ra_s, ra_r, rb_s, rb_r, bk_s, bk_r, xs_s, xs_r, sr_s, sr_r, fn_s, fn_r,
):
    gx = lax.axis_index("gx")
    gy = lax.axis_index("gy")
    j, q = gy // 4, gy % 4
    ylo, z = gx // 8, gx % 8
    sib = gy + 1 - 2 * (gy % 2)
    nbr = gy + 2 - 4 * ((gy // 2) % 2)
    qs, qn = sib % 4, nbr % 4
    qsn = (qs + 2) % 4
    ypart = (gx + 8) % NX

    def peer(r):
        return (gy + r) % NY

    def remote(src, dst, send, recv, tx, ty):
        return pltpu.make_async_remote_copy(
            src_ref=src, dst_ref=dst, send_sem=send, recv_sem=recv,
            device_id=(tx, ty), device_id_type=MESH,
        )

    def shift(k, u):
        return 8 * u + (3 * k + 4) % 8 if NS == 2 else 4 * u + (k + 3) % 4

    def loads():
        for i in range(16):
            p = (i % 4) * 4 + i // 4
            yield pltpu.make_async_copy(
                win_hbm.at[:, pl.ds(i * B, B)], win.at[:, pl.ds(p * B, B)], ld_sem.at[0, i]
            )
            yield pltpu.make_async_copy(
                wout_hbm.at[:, pl.ds(i * B, B)], wout.at[i % 4, :, pl.ds((i // 4) * B, B)], ld_sem.at[1, i]
            )

    for copy in loads():
        copy.start()

    barrier = pltpu.get_barrier_semaphore()
    for r in range(1, NX):
        pl.semaphore_signal(barrier, inc=1, device_id=((gx + r) % NX, gy), device_id_type=MESH)
    for r in range(1, 8):
        pl.semaphore_signal(barrier, inc=1, device_id=(gx, peer(2 * r)), device_id_type=MESH)
    pl.semaphore_signal(barrier, inc=1, device_id=(gx, sib), device_id_type=MESH)

    expert = 4 * lax.broadcasted_iota(jnp.int32, (NX, TOK), 0) + j
    named = jnp.zeros((NX, TOK), F32)
    weight = jnp.zeros((NX, TOK), F32)
    for k in range(TOPK):
        hit = idst[k : k + 1, :] == expert
        named = jnp.where(hit, 1.0, named)
        weight = jnp.where(hit, gatet[k : k + 1, :], weight)
    before = (
        lax.broadcasted_iota(jnp.int32, (TOK, TOK), 0) < lax.broadcasted_iota(jnp.int32, (TOK, TOK), 1)
    )
    count = jnp.dot(
        named.astype(BF16), jnp.where(before, 1.0, 0.0).astype(BF16), preferred_element_type=F32
    )
    code[...] = jnp.where(named > 0.0, count, -1.0)
    gm[...] = weight
    slot = lax.broadcasted_iota(jnp.int32, (CAP, TOK), 0).astype(F32)

    def build(k, carry):
        for u in range(NS):
            m = (gx + shift(k, u)) % NX
            hit = slot == code[pl.ds(m, 1), :]
            at = pl.multiple_of((NS * k + u) * CAP, CAP)
            oh[pl.ds(at, CAP), :] = jnp.where(hit, 1.0, 0.0).astype(BF16)
            og[pl.ds(at, CAP), :] = jnp.where(hit, gm[pl.ds(m, 1), :], 0.0).astype(BF16)
        return carry

    lax.fori_loop(0, NC, build, 0)

    pl.semaphore_wait(barrier, NX - 1 + 8)

    def tok_at(owner):
        return xall.at[owner % 4, :, pl.ds(pl.multiple_of((owner // 4) * B, B), B)]

    def tok_send(r):
        return remote(tok, tok_at(gy), tok_s.at[r], tok_r.at[r], gx, peer(2 * r))

    def tok_recv(r):
        place = tok_at(peer(16 - 2 * r))
        return remote(place, place, tok_s.at[r], tok_r.at[r], gx, sib)

    def tok_forward(r):
        place = tok_at(peer(16 - 2 * r))
        return remote(place, place, tf_s.at[r], tf_r.at[r], gx, sib)

    def tok_forwarded(r):
        place = tok_at((sib + 16 - 2 * r) % NY)
        return remote(place, place, tf_s.at[r], tf_r.at[r], gx, sib)

    tok_own = remote(tok, tok_at(gy), tf_s.at[0], tf_r.at[0], gx, sib)
    for r in (2, 4, 6):
        tok_send(r).start()

    def block_z(e):
        if e == 0:
            return z
        step = (e + 1) // 2
        return (z + 8 - step) % 8 if e % 2 else (z + step) % 8

    def w_at(owner):
        place = (owner % 4) * 4 + owner // 4
        return (
            wsin.at[:, :, pl.ds(pl.multiple_of(place * B, B), B)],
            wsout.at[owner % 4, :, pl.ds(pl.multiple_of((owner // 4) * B, B), B)],
        )

    def w_source(e):
        return (shin, shout) if e == 0 else w_at(ylo * 8 + block_z(e))

    def w_ring(e):
        origin = 0 if e <= 2 else e - 2
        target = ylo * 8 + ((z + 1) % 8 if e % 2 else (z + 7) % 8)
        to = w_at(ylo * 8 + block_z(origin))
        return [
            remote(w_source(origin)[t], to[t], wz_s.at[t, e], wz_r.at[t, e], target, gy) for t in range(2)
        ]

    def w_ring_recv(e):
        place = w_at(ylo * 8 + block_z(e))
        return [remote(place[t], place[t], wz_s.at[t, e], wz_r.at[t, e], ypart, gy) for t in range(2)]

    def w_cross(e):
        to = w_at(ylo * 8 + block_z(e))
        return [remote(w_source(e)[t], to[t], wy_s.at[t, e], wy_r.at[t, e], ypart, gy) for t in range(2)]

    def w_cross_recv(e):
        place = w_at((1 - ylo) * 8 + block_z(e))
        return [remote(place[t], place[t], wy_s.at[t, e], wy_r.at[t, e], ypart, gy) for t in range(2)]

    def start(copies):
        for copy in copies:
            copy.start()

    def arrived(copies):
        for copy in copies:
            copy.wait_recv()

    start(w_ring(1))
    start(w_ring(2))
    tok_own.start()
    for r in (1, 3, 5, 7):
        tok_send(r).start()
    start(w_cross(0))

    xall[q, :, pl.ds(pl.multiple_of(j * B, B), B)] = tok[...]
    wsin[:, :, pl.ds(pl.multiple_of(((gx % 4) * 4 + gx // 4) * B, B), B)] = shin[...]
    wsout[gx % 4, :, pl.ds(pl.multiple_of((gx // 4) * B, B), B)] = shout[...]

    def slots_of(k, u):
        return pl.ds(pl.multiple_of((NS * k + u) * CAP, CAP), CAP)

    def chunk_of(k):
        return pl.ds(pl.multiple_of(k * CH, CH), CH)

    def dp(k, u):
        return remote(
            snd.at[slots_of(k, u), :], rx.at[q, slots_of(k, u), :],
            dp_s.at[NS * k + u], dp_r.at[NS * k + u], (gx + shift(k, u)) % NX, gy,
        )

    def when_self(k, u, own, other):
        if u == 0:
            pl.when(k == SELF)(own)
            pl.when(k != SELF)(other)
        else:
            other()

    for e in (1, 2):
        arrived(w_ring_recv(e))
        start(w_ring(e + 2))
    for r in (2, 4, 6):
        tok_recv(r).wait_recv()

    def dispatch(k, carry):
        picked = jnp.dot(oh[chunk_of(k), :], xall[q], preferred_element_type=F32)
        snd[chunk_of(k), :] = picked.astype(BF16)
        for u in range(NS):
            def own(u=u):
                pltpu.make_async_copy(
                    snd.at[slots_of(k, u), :], rx.at[q, slots_of(k, u), :], dp_r.at[NS * k + u]
                ).start()

            when_self(k, u, own, lambda u=u: dp(k, u).start())
        return carry

    lax.fori_loop(0, NC, dispatch, 0)

    def to_nbr(k):
        place = rx.at[q, chunk_of(k), :]
        return remote(place, place, nb_s.at[k], nb_r.at[k], gx, nbr)

    def from_nbr(k):
        place = rx.at[qn, chunk_of(k), :]
        return remote(place, place, nb_s.at[k], nb_r.at[k], gx, nbr)

    def to_sib(t, k):
        place = rx.at[q if t == 0 else qn, chunk_of(k), :]
        return remote(place, place, sq_s.at[t, k], sq_r.at[t, k], gx, sib)

    def from_sib(t, k):
        place = rx.at[qs if t == 0 else qsn, chunk_of(k), :]
        return remote(place, place, sq_s.at[t, k], sq_r.at[t, k], gx, sib)

    def stage_a(k):
        for u in range(NS):
            place = rx.at[q, slots_of(k, u), :]
            remote(place, place, dp_s.at[NS * k + u], dp_r.at[NS * k + u], gx, sib).wait_recv()
        to_nbr(k).start()
        to_sib(0, k).start()

    def stage_a2(k):
        from_nbr(k).wait_recv()
        to_sib(1, k).start()

    def ra(k):
        return remote(sa.at[k], sibin.at[k], ra_s.at[k], ra_r.at[k], gx, sib)

    def rb(k):
        return remote(sn.at[k], nbrin.at[k], rb_s.at[k], rb_r.at[k], gx, nbr)

    def bk(k, u):
        return remote(
            ret.at[slots_of(k, u), :], back.at[slots_of(k, u), :],
            bk_s.at[NS * k + u], bk_r.at[NS * k + u], (gx + NX - shift(k, u)) % NX, gy,
        )

    def dot_nt(a, b):
        return lax.dot_general(a, b, (((1,), (1,)), ((), ())), preferred_element_type=F32)

    def normalise(source, rows, size):
        total = jnp.zeros((size, B), F32)
        for c in range(4):
            for b in range(4):
                value = source[c, rows, b * B : (b + 1) * B].astype(F32)
                total = total + value * value
        inverse = lax.rsqrt(jnp.sum(total, axis=1, keepdims=True) * (1.0 / D) + EPSILON)
        for c in range(4):
            for b in range(4):
                value = source[c, rows, b * B : (b + 1) * B].astype(F32)
                scaled = value * inverse * gain[4 * b + c : 4 * b + c + 1, :]
                xn[:size, c * Q + b * B : c * Q + (b + 1) * B] = scaled.astype(BF16)

    def stage_b(k):
        from_sib(0, k).wait_recv()
        from_sib(1, k).wait_recv()
        normalise(rx, chunk_of(k), CH)
        gate, up = dot_nt(xn[:CH, :], win[:PART, :]), dot_nt(xn[:CH, :], win[PART:, :])
        hidden = (jax.nn.silu(gate) * up).astype(BF16)
        sa[k, 0] = jnp.dot(hidden, wout[qs], preferred_element_type=F32).astype(BF16)
        sa[k, 1] = jnp.dot(hidden, wout[qsn], preferred_element_type=F32).astype(BF16)
        ra(k).start()
        pn[k] = jnp.dot(hidden, wout[qn], preferred_element_type=F32)
        po[k] = jnp.dot(hidden, wout[q], preferred_element_type=F32)

    def stage_rb(k):
        remote(sa.at[k], sibin.at[k], ra_s.at[k], ra_r.at[k], gx, sib).wait_recv()
        sn[k] = (pn[k] + sibin[k, 1].astype(F32)).astype(BF16)
        rb(k).start()
        po[k] = po[k] + sibin[k, 0].astype(F32)

    def stage_c(k):
        remote(sn.at[k], nbrin.at[k], rb_s.at[k], rb_r.at[k], gx, nbr).wait_recv()
        ret[chunk_of(k), :] = (po[k] + nbrin[k].astype(F32)).astype(BF16)
        for u in range(NS):
            def own(u=u):
                pltpu.make_async_copy(
                    ret.at[slots_of(k, u), :], back.at[slots_of(k, u), :], bk_r.at[NS * k + u]
                ).start()

            when_self(k, u, own, lambda u=u: bk(k, u).start())

    def ring_a():
        for e in (3, 4):
            arrived(w_ring_recv(e))
            start(w_ring(e + 2))
        for e in (1, 2):
            start(w_cross(e))

    def ring_b():
        for e in (5, 6):
            arrived(w_ring_recv(e))
        start(w_ring(7))
        for e in (3, 4):
            start(w_cross(e))

    def ring_c():
        arrived(w_ring_recv(7))
        for e in (5, 6, 7):
            start(w_cross(e))

    def others():
        for r in (2, 4, 6):
            tok_forward(r).start()
        for r in (1, 3, 5, 7):
            tok_recv(r).wait_recv()
            tok_forward(r).start()

    AHEAD = 2 if NS == 2 else 1
    for k in range(AHEAD):
        stage_a(k)
    others()
    ring_a()
    stage_a2(0)
    for copy in loads():
        copy.wait()

    def routed(it, carry):
        @pl.when(it < NC - AHEAD)
        def _():
            stage_a(it + AHEAD)

        @pl.when(it < NC - 1)
        def _():
            stage_a2(it + 1)

        stage_b(it)

        @pl.when(it > 0)
        def _():
            stage_rb(it - 1)

        pl.when(it == NC // 4)(ring_b)
        pl.when(it == NC // 2)(ring_c)
        return carry

    lax.fori_loop(0, NC, routed, 0)
    stage_rb(NC - 1)

    def rows_of(c):
        return pl.ds(pl.multiple_of(c * SH, SH), SH)

    tok_forwarded(0).wait_recv()
    for r in range(1, 8):
        tok_forwarded(r).wait_recv()
    for e in range(8):
        arrived(w_cross_recv(e))

    def xs(c):
        return remote(ssa.at[c], ssin.at[c], xs_s.at[c], xs_r.at[c], gx, sib)

    def sr(c, r):
        target = peer(2 * r)
        return remote(
            sb.at[r % 2, rows_of(c), pl.ds(pl.multiple_of((target // 4) * B, B), B)], shr.at[r, rows_of(c), :],
            sr_s.at[c, r], sr_r.at[c, r], gx, target,
        )

    def shared(c):
        rows = rows_of(c)
        normalise(xall, rows, SH)
        gate, up = dot_nt(xn[...], wsin[0]), dot_nt(xn[...], wsin[1])
        hidden = (jax.nn.silu(gate) * up).astype(BF16)
        ssa[c, 0] = jnp.dot(hidden, wsout[qs], preferred_element_type=F32).astype(BF16)
        ssa[c, 1] = jnp.dot(hidden, wsout[qsn], preferred_element_type=F32).astype(BF16)
        xs(c).start()
        spo[rows, :] = jnp.dot(hidden, wsout[q], preferred_element_type=F32)
        spn[rows, :] = jnp.dot(hidden, wsout[qn], preferred_element_type=F32)

    def fold(c):
        rows = rows_of(c)
        xs(c).wait_recv()
        own = spo[rows, :] + ssin[c, 0].astype(F32)
        spo[rows, :] = own
        sb[0, rows, :] = own.astype(BF16)
        sb[1, rows, :] = (spn[rows, :] + ssin[c, 1].astype(F32)).astype(BF16)
        for r in range(1, 8):
            sr(c, r).start()

    STEP = NC // 4

    def finish(k, carry):
        stage_c(k)
        part = k // STEP
        pl.when((k % STEP == STEP - 1) & (part % 2 == 0))(lambda: shared(part // 2))
        pl.when((k % STEP == STEP - 1) & (part % 2 == 1))(lambda: fold(part // 2))
        return carry

    lax.fori_loop(0, NC, finish, 0)

    acc[...] = jnp.zeros((TOK, Q), F32)

    def combine(k, carry):
        for u in range(4):
            i = 4 * k + u
            bk(i // NS, i % NS).wait_recv()
        rows = rows_of(k)
        acc[...] += lax.dot_general(
            og[rows, :], back[rows, :], (((0,), (0,)), ((), ())), preferred_element_type=F32
        )
        return carry

    lax.fori_loop(0, 4, combine, 0)

    def fn(t):
        return remote(fs.at[t], fin.at[t], fn_s.at[t], fn_r.at[t], gx, peer(4 * t))

    for t in range(1, 4):
        at = pl.multiple_of(((j + t) % 4) * B, B)
        fs[t] = acc[:, pl.ds(at, B)].astype(BF16)
        fn(t).start()
    mine = pl.ds(pl.multiple_of(j * B, B), B)
    total = acc[:, mine] + spo[:, mine]
    for r in range(1, 8):
        for c in range(2):
            sr(c, r).wait_recv()
        total = total + shr[r].astype(F32)
    for t in range(1, 4):
        fn(t).wait_recv()
        total = total + fin[t].astype(F32)
    out[...] = total.astype(BF16)

    tok_own.wait_send()
    for r in range(1, 8):
        tok_send(r).wait_send()
        tok_forward(r).wait_send()
        for c in range(2):
            sr(c, r).wait_send()
        for copy in w_ring(r):
            copy.wait_send()
    for e in range(8):
        for copy in w_cross(e):
            copy.wait_send()
    for c in range(2):
        xs(c).wait_send()
    for t in range(1, 4):
        fn(t).wait_send()

    def drain(k, carry):
        to_nbr(k).wait_send()
        to_sib(0, k).wait_send()
        to_sib(1, k).wait_send()
        ra(k).wait_send()
        rb(k).wait_send()
        for u in range(NS):
            def both(u=u):
                dp(k, u).wait_send()
                bk(k, u).wait_send()

            when_self(k, u, lambda: None, both)
        return carry

    lax.fori_loop(0, NC, drain, 0)


def on_device(tokens, norm_gain, expert_ids, gate_weights, shared_in, shared_out, expert_in, expert_out):
    dma = pltpu.SemaphoreType.DMA
    vmem = pl.BlockSpec(memory_space=pltpu.VMEM)
    anywhere = pl.BlockSpec(memory_space=pl.ANY)
    return pl.pallas_call(
        kernel,
        out_shape=jax.ShapeDtypeStruct((TOK, B), BF16),
        in_specs=[vmem] * 6 + [anywhere] * 2,
        out_specs=vmem,
        scratch_shapes=[
            pltpu.VMEM((4, TOK, Q), BF16),
            pltpu.VMEM((2 * PART, D), BF16),
            pltpu.VMEM((4, PART, Q), BF16),
            pltpu.VMEM((2, SPART, D), BF16),
            pltpu.VMEM((4, SPART, Q), BF16),
            pltpu.VMEM((NX, TOK), F32),
            pltpu.VMEM((NX, TOK), F32),
            pltpu.VMEM((NX * CAP, TOK), BF16),
            pltpu.VMEM((NX * CAP, TOK), BF16),
            pltpu.VMEM((NX * CAP, Q), BF16),
            pltpu.VMEM((4, NX * CAP, Q), BF16),
            pltpu.VMEM((SH, D), BF16),
            pltpu.VMEM((NC, 2, CH, Q), BF16),
            pltpu.VMEM((NC, 2, CH, Q), BF16),
            pltpu.VMEM((NC, CH, Q), F32),
            pltpu.VMEM((NC, CH, Q), F32),
            pltpu.VMEM((NC, CH, Q), BF16),
            pltpu.VMEM((NC, CH, Q), BF16),
            pltpu.VMEM((NX * CAP, Q), BF16),
            pltpu.VMEM((NX * CAP, Q), BF16),
            pltpu.VMEM((TOK, Q), F32),
            pltpu.VMEM((4, TOK, B), BF16),
            pltpu.VMEM((4, TOK, B), BF16),
            pltpu.VMEM((2, 2, SH, Q), BF16),
            pltpu.VMEM((2, 2, SH, Q), BF16),
            pltpu.VMEM((TOK, Q), F32),
            pltpu.VMEM((TOK, Q), F32),
            pltpu.VMEM((2, TOK, Q), BF16),
            pltpu.VMEM((8, TOK, B), BF16),
            dma((2, 16)),
            dma((8,)), dma((8,)),
            dma((8,)), dma((8,)),
            dma((2, 8)), dma((2, 8)),
            dma((2, 8)), dma((2, 8)),
            dma((16,)), dma((16,)),
            dma((NC,)), dma((NC,)),
            dma((2, NC)), dma((2, NC)),
            dma((NC,)), dma((NC,)),
            dma((NC,)), dma((NC,)),
            dma((16,)), dma((16,)),
            dma((2,)), dma((2,)),
            dma((2, 8)), dma((2, 8)),
            dma((4,)), dma((4,)),
        ],
        compiler_params=pltpu.CompilerParams(
            collective_id=0, has_side_effects=True, vmem_limit_bytes=VMEM_LIMIT
        ),
    )(
        tokens, norm_gain.reshape(D // B, B), expert_ids.T, gate_weights.T,
        jnp.swapaxes(shared_in, 1, 2), shared_out,
        expert_in.reshape(D, 2 * PART).T, expert_out.reshape(PART, D),
    )


def solution(mesh):
    in_specs = (
        P("gx", "gy"),
        P(),
        P("gx", None),
        P("gx", None),
        P(None, "gx", "gy"),
        P("gy", "gx"),
        P(("gx", "gy"), None, None),
        P(("gx", "gy"), None, None),
    )
    return jax.shard_map(
        on_device, mesh=mesh, in_specs=in_specs, out_specs=P("gx", "gy"), check_vma=False
    )
```

time: 148 us -> 123 us (0.83)
  the two profiles are of different devices: /device:TPU:37 before, /device:TPU:4 now
where the time goes in v3:
time: 123 us
  Pallas kernels  121 us (98%)
  local copies, waits for them, and re-layouts  1.57 us (1%)
    pallas_call x1, Pallas kernels, on_device(): pl.pallas_call(kernel, out_shape=jax.ShapeDtypeStruct((TOK, B), BF16), in...  121 us

profile of v3, /device:TPU:4, one launch (start us, length us, event | category | flops | bytes accessed | tf_op | source)
XLA Modules:
  0.0 122.6 jit_solution(2026272372836051280)
XLA Ops:
  0.0 121.0 %shard_map.82 = bf16[512,128]{1,0:T(8,128)(2,1)} custom-call(bf16[512,128]{1,0:T(8,128)(2,1)} %tok.1, f32[16,128]{1,0:T(8,128)} %bitcast.13, s32[6,512]{1,0:T(8,128)} %bitcast.11, f32[6,512]{1,0:T(8,128)} %bitcast.12, bf16[2,176,128]{2,1,0:T(8,128)(2,1)} %bitcast.10, bf16[176,128]{1,0:T(8,128)(2,1)} %shout.1, bf16[704,2048]{1,0:T(8,128)(2,1)} %bitcast.8, ...), custom_call_target="tpu_custom_call" | custom-call | tf_op jit(solution)/shard_map/pallas_call | solution.py:487
  121.0 1.6 %copy.10 = bf16[512,128]{1,0:T(8,128)(2,1)} copy(bf16[512,128]{1,0:T(8,128)(2,1)} %shard_map.82) | data formatting | bytes 262144

commit v4 on v3

--- a/solution.py
+++ b/solution.py
@@ -23,9 +23,27 @@
 NS = 2
 NC = NX // NS
 CH = NS * CAP
-SELF = 4 if NS == 2 else 1
 SH = 256
 VMEM_LIMIT = 60 * 1024 * 1024
+
+
+SEND = (0, 1, 7, 2, 6, 3, 5, 4)
+PLAN = (
+    "A0 A1 A7 O",
+    "W1 N0 B0 A2",
+    "A6 N1 B1 W2",
+    "N7 B7 R0 N2",
+    "B2 W3 A3 A5",
+    "R1 N6 B6 A4",
+    "R2 N3 B3 R6",
+    "N5 B5 R3 C0",
+    "N4 B4 R5 C1",
+    "R4 R7 C2 C6",
+    "S0 C3 C5 S1",
+    "F0 C4 C7 F1",
+    "G0 G1 G2 G6",
+    "G3 G5 G4 G7",
+)
 
 
 def kernel(
@@ -55,7 +73,7 @@
         )
 
     def shift(k, u):
-        return 8 * u + (3 * k + 4) % 8 if NS == 2 else 4 * u + (k + 3) % 4
+        return 8 * u + k
 
     def loads():
         for i in range(16):
@@ -94,16 +112,13 @@
     gm[...] = weight
     slot = lax.broadcasted_iota(jnp.int32, (CAP, TOK), 0).astype(F32)
 
-    def build(k, carry):
+    for k in range(NC):
         for u in range(NS):
             m = (gx + shift(k, u)) % NX
             hit = slot == code[pl.ds(m, 1), :]
-            at = pl.multiple_of((NS * k + u) * CAP, CAP)
-            oh[pl.ds(at, CAP), :] = jnp.where(hit, 1.0, 0.0).astype(BF16)
-            og[pl.ds(at, CAP), :] = jnp.where(hit, gm[pl.ds(m, 1), :], 0.0).astype(BF16)
-        return carry
-
-    lax.fori_loop(0, NC, build, 0)
+            at = pl.ds((NS * k + u) * CAP, CAP)
+            oh[at, :] = jnp.where(hit, 1.0, 0.0).astype(BF16)
+            og[at, :] = jnp.where(hit, gm[pl.ds(m, 1), :], 0.0).astype(BF16)
 
     pl.semaphore_wait(barrier, NX - 1 + 8)
 
@@ -185,10 +200,10 @@
     wsout[gx % 4, :, pl.ds(pl.multiple_of((gx // 4) * B, B), B)] = shout[...]
 
     def slots_of(k, u):
-        return pl.ds(pl.multiple_of((NS * k + u) * CAP, CAP), CAP)
+        return pl.ds((NS * k + u) * CAP, CAP)
 
     def chunk_of(k):
-        return pl.ds(pl.multiple_of(k * CH, CH), CH)
+        return pl.ds(k * CH, CH)
 
     def dp(k, u):
         return remote(
@@ -196,32 +211,24 @@
             dp_s.at[NS * k + u], dp_r.at[NS * k + u], (gx + shift(k, u)) % NX, gy,
         )
 
-    def when_self(k, u, own, other):
-        if u == 0:
-            pl.when(k == SELF)(own)
-            pl.when(k != SELF)(other)
-        else:
-            other()
-
     for e in (1, 2):
         arrived(w_ring_recv(e))
         start(w_ring(e + 2))
     for r in (2, 4, 6):
         tok_recv(r).wait_recv()
 
-    def dispatch(k, carry):
+    for k in SEND:
         picked = jnp.dot(oh[chunk_of(k), :], xall[q], preferred_element_type=F32)
         snd[chunk_of(k), :] = picked.astype(BF16)
         for u in range(NS):
-            def own(u=u):
+            if shift(k, u):
+                dp(k, u).start()
+            else:
                 pltpu.make_async_copy(
                     snd.at[slots_of(k, u), :], rx.at[q, slots_of(k, u), :], dp_r.at[NS * k + u]
                 ).start()
-
-            when_self(k, u, own, lambda u=u: dp(k, u).start())
-        return carry
-
-    lax.fori_loop(0, NC, dispatch, 0)
+    for e in (1, 2):
+        start(w_cross(e))
 
     def to_nbr(k):
         place = rx.at[q, chunk_of(k), :]
@@ -300,31 +307,24 @@
         remote(sn.at[k], nbrin.at[k], rb_s.at[k], rb_r.at[k], gx, nbr).wait_recv()
         ret[chunk_of(k), :] = (po[k] + nbrin[k].astype(F32)).astype(BF16)
         for u in range(NS):
-            def own(u=u):
+            if shift(k, u):
+                bk(k, u).start()
+            else:
                 pltpu.make_async_copy(
                     ret.at[slots_of(k, u), :], back.at[slots_of(k, u), :], bk_r.at[NS * k + u]
                 ).start()
 
-            when_self(k, u, own, lambda u=u: bk(k, u).start())
-
-    def ring_a():
-        for e in (3, 4):
-            arrived(w_ring_recv(e))
-            start(w_ring(e + 2))
-        for e in (1, 2):
-            start(w_cross(e))
-
-    def ring_b():
-        for e in (5, 6):
-            arrived(w_ring_recv(e))
-        start(w_ring(7))
-        for e in (3, 4):
-            start(w_cross(e))
-
-    def ring_c():
-        arrived(w_ring_recv(7))
-        for e in (5, 6, 7):
-            start(w_cross(e))
+    def ring(n):
+        if n < 3:
+            for e in (2 * n + 1, 2 * n + 2):
+                arrived(w_ring_recv(e))
+                if e + 2 < 8:
+                    start(w_ring(e + 2))
+            for e in (2 * n + 1, 2 * n + 2):
+                start(w_cross(e))
+        else:
+            arrived(w_ring_recv(7))
+            start(w_cross(7))
 
     def others():
         for r in (2, 4, 6):
@@ -333,45 +333,8 @@
             tok_recv(r).wait_recv()
             tok_forward(r).start()
 
-    AHEAD = 2 if NS == 2 else 1
-    for k in range(AHEAD):
-        stage_a(k)
-    others()
-    ring_a()
-    stage_a2(0)
-    for copy in loads():
-        copy.wait()
-
-    def routed(it, carry):
-        @pl.when(it < NC - AHEAD)
-        def _():
-            stage_a(it + AHEAD)
-
-        @pl.when(it < NC - 1)
-        def _():
-            stage_a2(it + 1)
-
-        stage_b(it)
-
-        @pl.when(it > 0)
-        def _():
-            stage_rb(it - 1)
-
-        pl.when(it == NC // 4)(ring_b)
-        pl.when(it == NC // 2)(ring_c)
-        return carry
-
-    lax.fori_loop(0, NC, routed, 0)
-    stage_rb(NC - 1)
-
     def rows_of(c):
         return pl.ds(pl.multiple_of(c * SH, SH), SH)
-
-    tok_forwarded(0).wait_recv()
-    for r in range(1, 8):
-        tok_forwarded(r).wait_recv()
-    for e in range(8):
-        arrived(w_cross_recv(e))
 
     def xs(c):
         return remote(ssa.at[c], ssin.at[c], xs_s.at[c], xs_r.at[c], gx, sib)
@@ -384,6 +347,11 @@
         )
 
     def shared(c):
+        if c == 0:
+            for r in range(8):
+                tok_forwarded(r).wait_recv()
+            for e in range(8):
+                arrived(w_cross_recv(e))
         rows = rows_of(c)
         normalise(xall, rows, SH)
         gate, up = dot_nt(xn[...], wsin[0]), dot_nt(xn[...], wsin[1])
@@ -404,30 +372,32 @@
         for r in range(1, 8):
             sr(c, r).start()
 
-    STEP = NC // 4
-
-    def finish(k, carry):
-        stage_c(k)
-        part = k // STEP
-        pl.when((k % STEP == STEP - 1) & (part % 2 == 0))(lambda: shared(part // 2))
-        pl.when((k % STEP == STEP - 1) & (part % 2 == 1))(lambda: fold(part // 2))
-        return carry
-
-    lax.fori_loop(0, NC, finish, 0)
-
-    acc[...] = jnp.zeros((TOK, Q), F32)
-
-    def combine(k, carry):
-        for u in range(4):
-            i = 4 * k + u
-            bk(i // NS, i % NS).wait_recv()
-        rows = rows_of(k)
-        acc[...] += lax.dot_general(
+    summed = []
+
+    def combine(k):
+        for u in range(NS):
+            bk(k, u).wait_recv()
+        rows = chunk_of(k)
+        part = lax.dot_general(
             og[rows, :], back[rows, :], (((0,), (0,)), ((), ())), preferred_element_type=F32
         )
-        return carry
-
-    lax.fori_loop(0, 4, combine, 0)
+        acc[...] = acc[...] + part if summed else part
+        summed.append(k)
+
+    steps = {
+        "A": stage_a, "N": stage_a2, "B": stage_b, "R": stage_rb, "C": stage_c, "G": combine,
+        "S": shared, "F": fold, "W": ring,
+    }
+    loaded = False
+    for step in " ".join(PLAN).split():
+        if step == "O":
+            others()
+            continue
+        if step[0] == "B" and not loaded:
+            for copy in loads():
+                copy.wait()
+            loaded = True
+        steps[step[0]](int(step[1:]))
 
     def fn(t):
         return remote(fs.at[t], fin.at[t], fn_s.at[t], fn_r.at[t], gx, peer(4 * t))
@@ -463,21 +433,16 @@
     for t in range(1, 4):
         fn(t).wait_send()
 
-    def drain(k, carry):
+    for k in range(NC):
         to_nbr(k).wait_send()
         to_sib(0, k).wait_send()
         to_sib(1, k).wait_send()
         ra(k).wait_send()
         rb(k).wait_send()
         for u in range(NS):
-            def both(u=u):
+            if shift(k, u):
                 dp(k, u).wait_send()
                 bk(k, u).wait_send()
-
-            when_self(k, u, lambda: None, both)
-        return carry
-
-    lax.fori_loop(0, NC, drain, 0)
 
 
 def on_device(tokens, norm_gain, expert_ids, gate_weights, shared_in, shared_out, expert_in, expert_out):

time: 123 us -> 117 us (0.951)
  the two profiles are of different devices: /device:TPU:4 before, /device:TPU:14 now
where the time goes in v4:
time: 117 us
  Pallas kernels  115 us (98%)
  local copies, waits for them, and re-layouts  1.57 us (1%)
    pallas_call x1, Pallas kernels, on_device(): pl.pallas_call(kernel, out_shape=jax.ShapeDtypeStruct((TOK, B), BF16), in...  115 us

profile of v4, /device:TPU:14, one launch (start us, length us, event | category | flops | bytes accessed | tf_op | source)
XLA Modules:
  0.0 116.7 jit_solution(13200265383764168853)
XLA Ops:
  0.0 115.1 %shard_map.82 = bf16[512,128]{1,0:T(8,128)(2,1)} custom-call(bf16[512,128]{1,0:T(8,128)(2,1)} %tok.1, f32[16,128]{1,0:T(8,128)} %bitcast.13, s32[6,512]{1,0:T(8,128)} %bitcast.11, f32[6,512]{1,0:T(8,128)} %bitcast.12, bf16[2,176,128]{2,1,0:T(8,128)(2,1)} %bitcast.10, bf16[176,128]{1,0:T(8,128)(2,1)} %shout.1, bf16[704,2048]{1,0:T(8,128)(2,1)} %bitcast.8, ...), custom_call_target="tpu_custom_call" | custom-call | tf_op jit(solution)/shard_map/pallas_call | solution.py:452
  115.1 1.6 %copy.10 = bf16[512,128]{1,0:T(8,128)(2,1)} copy(bf16[512,128]{1,0:T(8,128)(2,1)} %shard_map.82) | data formatting | bytes 262144

commit v5 on v4

--- a/solution.py
+++ b/solution.py
@@ -38,9 +38,9 @@
     "R2 N3 B3 R6",
     "N5 B5 R3 C0",
     "N4 B4 R5 C1",
-    "R4 R7 C2 C6",
-    "S0 C3 C5 S1",
-    "F0 C4 C7 F1",
+    "R4 R7 S0 C2",
+    "C6 F0 S1 C3",
+    "C5 F1 C4 C7",
     "G0 G1 G2 G6",
     "G3 G5 G4 G7",
 )
@@ -190,10 +190,6 @@
 
     start(w_ring(1))
     start(w_ring(2))
-    tok_own.start()
-    for r in (1, 3, 5, 7):
-        tok_send(r).start()
-    start(w_cross(0))
 
     xall[q, :, pl.ds(pl.multiple_of(j * B, B), B)] = tok[...]
     wsin[:, :, pl.ds(pl.multiple_of(((gx % 4) * 4 + gx // 4) * B, B), B)] = shin[...]
@@ -216,6 +212,10 @@
         start(w_ring(e + 2))
     for r in (2, 4, 6):
         tok_recv(r).wait_recv()
+    tok_own.start()
+    for r in (1, 3, 5, 7):
+        tok_send(r).start()
+    start(w_cross(0))
 
     for k in SEND:
         picked = jnp.dot(oh[chunk_of(k), :], xall[q], preferred_element_type=F32)

time: 117 us -> 113 us (0.966)
  the two profiles are of different devices: /device:TPU:14 before, /device:TPU:39 now
where the time goes in v5:
time: 113 us; the launch traced here: 111 us
  Pallas kernels  110 us (97%)
  local copies, waits for them, and re-layouts  1.57 us (1%)
    pallas_call x1, Pallas kernels, on_device(): pl.pallas_call(kernel, out_shape=jax.ShapeDtypeStruct((TOK, B), BF16), in...  110 us

profile of v5, /device:TPU:39, one launch (start us, length us, event | category | flops | bytes accessed | tf_op | source)
XLA Modules:
  0.0 111.3 jit_solution(2136070040675150404)
XLA Ops:
  0.0 109.7 %shard_map.82 = bf16[512,128]{1,0:T(8,128)(2,1)} custom-call(bf16[512,128]{1,0:T(8,128)(2,1)} %tok.1, f32[16,128]{1,0:T(8,128)} %bitcast.13, s32[6,512]{1,0:T(8,128)} %bitcast.11, f32[6,512]{1,0:T(8,128)} %bitcast.12, bf16[2,176,128]{2,1,0:T(8,128)(2,1)} %bitcast.10, bf16[176,128]{1,0:T(8,128)(2,1)} %shout.1, bf16[704,2048]{1,0:T(8,128)(2,1)} %bitcast.8, ...), custom_call_target="tpu_custom_call" | custom-call | tf_op jit(solution)/shard_map/pallas_call | solution.py:452
  109.7 1.6 %copy.10 = bf16[512,128]{1,0:T(8,128)(2,1)} copy(bf16[512,128]{1,0:T(8,128)(2,1)} %shard_map.82) | data formatting | bytes 262144

commit v6 on v5

--- a/solution.py
+++ b/solution.py
@@ -32,17 +32,17 @@
     "A0 A1 A7 O",
     "W1 N0 B0 A2",
     "A6 N1 B1 W2",
-    "N7 B7 R0 N2",
+    "N7 B7 R1 N2",
     "B2 W3 A3 A5",
-    "R1 N6 B6 A4",
+    "R7 N6 B6 A4",
     "R2 N3 B3 R6",
-    "N5 B5 R3 C0",
-    "N4 B4 R5 C1",
-    "R4 R7 S0 C2",
+    "N5 B5 R3 C1",
+    "N4 B4 R5 C7",
+    "R4 R0 S0 C2",
     "C6 F0 S1 C3",
-    "C5 F1 C4 C7",
-    "G0 G1 G2 G6",
-    "G3 G5 G4 G7",
+    "C5 F1 C4 C0",
+    "G1 G7 G2 G6",
+    "G3 G5 G4 G0",
 )
 
 

time: 113 us -> 112 us (level); the launches traced: 111 us -> 112 us
  no operation moved by 1% of the time
where the time goes in v6:
time: 112 us
  Pallas kernels  110 us (98%)
  local copies, waits for them, and re-layouts  1.57 us (1%)
    pallas_call x1, Pallas kernels, on_device(): pl.pallas_call(kernel, out_shape=jax.ShapeDtypeStruct((TOK, B), BF16), in...  110 us

profile of v6, /device:TPU:39, one launch (start us, length us, event | category | flops | bytes accessed | tf_op | source)
XLA Modules:
  0.0 111.6 jit_solution(16384014497173808874)
XLA Ops:
  0.0 110.1 %shard_map.82 = bf16[512,128]{1,0:T(8,128)(2,1)} custom-call(bf16[512,128]{1,0:T(8,128)(2,1)} %tok.1, f32[16,128]{1,0:T(8,128)} %bitcast.13, s32[6,512]{1,0:T(8,128)} %bitcast.11, f32[6,512]{1,0:T(8,128)} %bitcast.12, bf16[2,176,128]{2,1,0:T(8,128)(2,1)} %bitcast.10, bf16[176,128]{1,0:T(8,128)(2,1)} %shout.1, bf16[704,2048]{1,0:T(8,128)(2,1)} %bitcast.8, ...), custom_call_target="tpu_custom_call" | custom-call | tf_op jit(solution)/shard_map/pallas_call | solution.py:452
  110.1 1.6 %copy.10 = bf16[512,128]{1,0:T(8,128)(2,1)} copy(bf16[512,128]{1,0:T(8,128)(2,1)} %shard_map.82) | data formatting | bytes 262144
